TPU v7x, 32 devices: a whole 2x2x4 slice. The times are simulated.
32 devices in a mesh: row: 4 (over y, x), col: 8 (over z, core).
Axes of the slice: x: 2, y: 2, z: 4, core: 2. Of those that a mesh axis runs over, the one named last changes fastest.
Arguments:
- coupling: float32 [4, 4608, 18432], P(None, 'col', 'row'), may hold values from -0.046875 to 0.046875
- energies: float32 [18432], P(('row', 'col')), may hold values from 0.7 to 14.2
- block: float32 [18432, 16], P(('row', 'col')), may hold values from -6 to 6
Outputs:
- basis: float32 [18432, 16], P(('row', 'col'))
- projections: float32 [2, 16, 16], replicated
- factors: float32 [2, 16, 16], replicated
All inputs are finite; a program needn't handle non-finite values.
Results may differ from a plain program's by a relative error of at most 0.0003.
Values sent between devices are 32-bit elements; how exact they have to be, the bound alone decides.
No kernel may reach another device: no remote copies, remote signals or barrier semaphores. Data moves between devices by JAX's collectives and lax.ppermute only.
A program may use at most 128 MiB of HBM per device.

v0:
```python
import jax
import jax.numpy as jnp
from jax import lax
from jax.sharding import PartitionSpec as P

N = 18432
ITERS = 2
precise = lax.Precision.HIGHEST


def combined(moments_local):
    return lax.psum(moments_local, "row")


def on_device(coupling, energies, block):
    segment = block.shape[0]
    width = block.shape[1]
    column = lax.axis_index("col")
    current, energy_rows = (
        lax.all_gather(block, "col", axis=0, tiled=True),
        lax.all_gather(energies, "col", axis=0, tiled=True),
    )
    prior = jnp.zeros_like(current)
    projection_list = []
    factor_list = []
    for section in range(ITERS):
        own_rows = lax.dynamic_slice_in_dim(current, column * segment, segment, 0)
        column_block = current
        spread = lax.all_gather(own_rows, "row", axis=0, tiled=True)
        spread = spread.reshape(coupling.shape[0], segment, width)
        direct = lax.psum_scatter(
            jnp.einsum("aig,gk->aik", coupling, column_block, precision=precise),
            "row",
            scatter_dimension=0,
            tiled=True,
        ).reshape(segment, width)
        partial_value = jnp.einsum("aig,aik->gk", coupling, spread, precision=precise)
        transposed = lax.psum(partial_value, "col")
        direct_rows = lax.all_gather(direct, "col", axis=0, tiled=True)
        product = energy_rows[:, None] * current + direct_rows + transposed
        stacked = jnp.concatenate([current, prior, product], axis=1)
        moments = combined(jnp.einsum("nk,nl->kl", stacked, stacked, precision=precise)) / N
        projection = moments[:width, 2 * width :]
        cross = moments[width : 2 * width, 2 * width :]
        weights = jnp.concatenate([-projection, -cross, jnp.eye(width, dtype=jnp.float32)], axis=0)
        gram_matrix = jnp.dot(
            weights.T, jnp.dot(moments, weights, precision=precise), precision=precise
        )
        factor = jnp.linalg.cholesky(gram_matrix)
        residual = (
            product
            - jnp.dot(current, projection, precision=precise)
            - jnp.dot(prior, cross, precision=precise)
        )
        prior = current
        current = jax.scipy.linalg.solve_triangular(factor, residual.T, lower=True).T
        projection_list.append(projection)
        factor_list.append(factor)
    basis = lax.dynamic_slice_in_dim(current, column * segment, segment, 0)
    return (basis, jnp.stack(projection_list), jnp.stack(factor_list))


def solution(mesh):
    placed = (P(None, "col", "row"), P(("row", "col")), P(("row", "col"), None))
    return jax.shard_map(
        on_device,
        mesh=mesh,
        in_specs=placed,
        out_specs=(P(("row", "col"), None), P(), P()),
        check_vma=False,
    )
```

profile of v0, /device:TPU:0, one launch (start us, length us, event | category | flops | bytes accessed | tf_op | source)
XLA Modules:
  0.0 340.6 jit_solution(8555709565530399333)
XLA Ops:
  8.0 16.3 %all-gather.2 = f32[8,576,16]{1,2,0:T(8,128)S(1)} all-gather(f32[1,576,16]{1,2,0:T(8,128)} %bitcast.93), channel_id=1, replica_groups=mesh['row'=4,'col'=8] {'col'}, dimensions={0}, use_global_device_ids=true | all-gather | bytes 331776 | tf_op jit(solution)/shard_map/all_gather | solution.py:20
  24.6 40.0 %fusion.44 = f32[4,576,16]{1,2,0:T(8,128)} fusion(f32[4,576,4608]{2,1,0:T(8,128)} %param.6, f32[4608,16,1]{0,1,2:T(8,128)S(1)} %reshape.46), kind=kOutput, calls=%fused_computation.77 | convolution fusion | flops 2038431744 | bytes 42909696 | tf_op jit(solution)/shard_map/aig,gk->aik/dot_general | solution.py:32
  64.9 8.8 %all-gather.3 = f32[4,576,16]{1,2,0:T(8,128)S(1)} all-gather(f32[1,576,16]{1,2,0:T(8,128)S(1)} %dynamic-slice_bitcast_fusion.2), channel_id=1, replica_groups=mesh['row'=4,'col'=8] {'row'}, dimensions={0}, use_global_device_ids=true | all-gather | bytes 184320 | tf_op jit(solution)/shard_map/all_gather | solution.py:29
  73.6 24.6 %convolution_bitcast_fusion.3 = f32[4608,16]{0,1:T(8,128)} fusion(f32[4,576,16]{1,2,0:T(8,128)S(1)} %all-gather.3, f32[4,576,4608]{2,1,0:T(8,128)} %param.6), kind=kOutput, calls=%fused_computation.9 | convolution fusion | flops 2038431744 | bytes 42909696 | tf_op jit(solution)/shard_map/aig,aik->gk/dot_general | solution.py:37
  99.9 27.3 %all-reduce = f32[4608]{0:T(1024)S(1)} all-reduce(f32[4608]{0:T(1024)S(1)} %dynamic-update-slice.2), channel_id=1, replica_groups=mesh['row'=4,'col'=8] {'col'}, use_global_device_ids=true, to_apply=%add | all-reduce | flops 4608 | bytes 36864
  127.2 0.9 copy.10
  128.2 24.6 %all-gather = f32[1,4608,16]{2,0,1:T(1,128)S(1)} all-gather(f32[1,576,16]{2,0,1:T(1,128)S(1)} %copy.10), channel_id=2, replica_groups=mesh['row'=4,'col'=8] {'col'}, dimensions={1}, use_global_device_ids=true | all-gather | bytes 331776 | tf_op jit(solution)/shard_map/all_gather | solution.py:39
  152.7 2.2 copy.11
  154.9 1.0 fusion.19
  156.0 0.9 fusion.5
  156.9 15.3 %psum.29 = f32[48,48]{1,0:T(8,128)S(1)} all-reduce(f32[48,48]{1,0:T(8,128)S(1)} %fusion.5), channel_id=1, replica_groups=mesh['row'=4,'col'=8] {'row'}, use_global_device_ids=true, to_apply=%region_2.0 | all-reduce | flops 2304 | bytes 18432 | tf_op jit(solution)/shard_map/psum | solution.py:12
  172.3 0.7 slice_bitcast_fusion.1
  173.6 1.5 cholesky.44
  175.1 0.6 compare_reduce_fusion.1
  175.7 0.6 fusion.37
  176.4 1.2 custom-call.6
  178.6 39.3 %convolution_bitcast_fusion.4 = f32[4,576,16]{1,2,0:T(8,128)} fusion(f32[4,576,4608]{2,1,0:T(8,128)} %param.6, f32[16,4608]{1,0:T(8,128)S(1)} %fusion.23), kind=kOutput, calls=%fused_computation.10 | convolution fusion | flops 2038431744 | bytes 42909696 | tf_op jit(solution)/shard_map/aig,gk->aik/dot_general | solution.py:32
  218.1 8.7 %all-gather.4 = f32[4,576,16]{1,2,0:T(8,128)S(1)} all-gather(f32[1,576,16]{1,2,0:T(8,128)S(1)} %dynamic-slice_bitcast_fusion.1), channel_id=1, replica_groups=mesh['row'=4,'col'=8] {'row'}, dimensions={0}, use_global_device_ids=true | all-gather | bytes 184320 | tf_op jit(solution)/shard_map/all_gather | solution.py:29
  226.8 24.6 %convolution_bitcast_fusion.2 = f32[4608,16]{0,1:T(8,128)} fusion(f32[4,576,16]{1,2,0:T(8,128)S(1)} %all-gather.4, f32[4,576,4608]{2,1,0:T(8,128)} %param.6), kind=kOutput, calls=%fused_computation.8 | convolution fusion | flops 2038431744 | bytes 42909696 | tf_op jit(solution)/shard_map/aig,aik->gk/dot_general | solution.py:37
  251.4 0.9 copy.15
  252.4 28.0 %all-gather.1 = f32[1,4608,16]{2,0,1:T(1,128)S(1)} all-gather(f32[1,576,16]{2,0,1:T(1,128)S(1)} %copy.15), channel_id=3, replica_groups=mesh['row'=4,'col'=8] {'col'}, dimensions={1}, use_global_device_ids=true | all-gather | bytes 331776 | tf_op jit(solution)/shard_map/all_gather | solution.py:39
  280.4 2.2 copy.16
  282.6 24.1 %all-reduce.8.cloned.1.call-done = f32[4608,16]{0,1:T(8,128)} async-done(((f32[4608,16]{0,1:T(8,128)}), f32[4608,16]{0,1:T(8,128)}) %all-reduce.8.cloned.1.call-update) | async-done | bytes 294928 | tf_op jit(solution)/shard_map/psum | solution.py:38
  306.7 1.1 fusion.17
  307.7 0.8 fusion.10
  308.6 16.3 %psum.31 = f32[48,48]{1,0:T(8,128)S(1)} all-reduce(f32[48,48]{1,0:T(8,128)S(1)} %fusion.10), channel_id=1, replica_groups=mesh['row'=4,'col'=8] {'row'}, use_global_device_ids=true, to_apply=%region_8.11 | all-reduce | flops 2304 | bytes 18432 | tf_op jit(solution)/shard_map/psum | solution.py:12
  326.1 1.5 cholesky.55
  327.6 0.6 compare_reduce_fusion
  328.3 0.6 fusion.36
  328.9 1.2 custom-call.7
  331.1 0.7 dynamic-slice_bitcast_fusion
  331.8 1.3 pad_maximum_fusion
  (50 shorter events, 5.6 us)
Async XLA Ops:
  8.0 119.2 %reduce-scatter.7.cloned.1.call-start = ((), (), s32[]{:S(2)}) async-start(), calls=%async_computation.4 | async-start | bytes 204800
  24.5 73.8 %copy-start.2 = (u32[32]{0:T(128)S(1)}, u32[32]{0:T(128)}, u32[]{:S(2)}) copy-start(u32[32]{0:T(128)} %constant.50) | copy-start | bytes 388
  24.5 75.1 %copy-start.1 = (f32[576]{0:T(1024)S(1)}, f32[576]{0:T(1024)}, u32[]{:S(2)}) copy-start(f32[576]{0:T(1024)} %param.7) | copy-start | bytes 6916
  64.6 90.3 %all-reduce.6.cloned.1.call-start = ((), (), s32[]{:S(2)}) async-start(), calls=%async_computation.2 | async-start | bytes 589824 | tf_op jit(solution)/shard_map/psum | solution.py:38
  98.3 153.2 %reduce-scatter.9.cloned.1.call-start = ((), (), s32[]{:S(2)}) async-start(), calls=%async_computation.5 | async-start | bytes 204800
  127.2 124.2 %copy-start = (f32[4608]{0:T(1024)}, f32[4608]{0:T(1024)S(1)}, u32[]{:S(2)}) copy-start(f32[4608]{0:T(1024)S(1)} %all-reduce) | copy-start | bytes 55300
  218.0 88.7 %all-reduce.8.cloned.1.call-start = ((), (), s32[]{:S(2)}) async-start(), calls=%async_computation.3 | async-start | bytes 589824 | tf_op jit(solution)/shard_map/psum | solution.py:38
Sparse Core Ops, SparseCore 0:
  64.7 25.2 reduce-scatter.6
  218.1 24.4 reduce-scatter.8
Sparse Core Ops, SparseCore 1:
  98.3 55.3 all-reduce.5
  251.5 55.1 all-reduce.7
where the time goes:
time: 341 us
  blocking collectives  145 us (43%)
  matrix products  134 us (39%)
  waiting for transfers between devices  24.2 us (7%)
  between operations  16.4 us (5%)
  other arithmetic  12.2 us (4%)
  local copies, waits for them, and re-layouts  8.71 us (3%)
    dot_general x2, matrix products, on_device(): jnp.einsum('aig,gk->aik', coupling, column_block, precision=precise)  79.3 us
    all_gather x2, blocking collectives, on_device(): direct_rows = lax.all_gather(direct, 'col', axis=0, tiled=True)  52.6 us
    dot_general x2, matrix products, on_device(): jnp.einsum('aig,aik->gk', coupling, spread, precision=precise)  49.2 us
    psum x2, blocking collectives, combined(): return lax.psum(moments_local, 'row')  31.6 us
    unnamed x1, blocking collectives  27.3 us
    psum x2, waiting for transfers between devices, on_device(): transposed = lax.psum(partial_value, 'col')  24.1 us
    all_gather x2, blocking collectives, on_device(): spread = lax.all_gather(own_rows, 'row', axis=0, tiled=True)  17.5 us
    all_gather x1, blocking collectives, on_device(): lax.all_gather(block, 'col', axis=0, tiled=True)  16.3 us
  transfers between devices with their start and end apart: 4, of which 1 were waited for; matrix products, arithmetic and copies ran while one was open for 17% of the time, Pallas kernels for 0%

commit v1 on v0

--- a/solution.py
+++ b/solution.py
@@ -9,7 +9,7 @@
 
 
 def combined(moments_local):
-    return lax.psum(moments_local, "row")
+    return jnp.sum(lax.all_gather(moments_local, "row"), axis=0)
 
 
 def on_device(coupling, energies, block):

time: 341 us -> 326 us (0.956)
  blocking collectives: 145 us -> 130 us
    psum x2 -> x0, blocking collectives: 31.6 us -> none  [combined(): return lax.psum(moments_local, 'row')]
    all_gather x0 -> x2, blocking collectives: none -> 16.8 us  [combined(): return jnp.sum(lax.all_gather(moments_local, 'row'), axis=0)]
where the time goes in v1:
time: 326 us
  matrix products  134 us (41%)
  blocking collectives  130 us (40%)
  waiting for transfers between devices  24.7 us (8%)
  between operations  16.4 us (5%)
  other arithmetic  12.2 us (4%)
  local copies, waits for them, and re-layouts  8.71 us (3%)
    dot_general x2, matrix products, on_device(): jnp.einsum('aig,gk->aik', coupling, column_block, precision=precise)  79.3 us
    all_gather x2, blocking collectives, on_device(): direct_rows = lax.all_gather(direct, 'col', axis=0, tiled=True)  52.6 us
    dot_general x2, matrix products, on_device(): jnp.einsum('aig,aik->gk', coupling, spread, precision=precise)  49.2 us
    unnamed x1, blocking collectives  27.3 us
    psum x2, waiting for transfers between devices, on_device(): transposed = lax.psum(partial_value, 'col')  24.6 us
    all_gather x2, blocking collectives, on_device(): spread = lax.all_gather(own_rows, 'row', axis=0, tiled=True)  16.8 us
    all_gather x2, blocking collectives, combined(): return jnp.sum(lax.all_gather(moments_local, 'row'), axis=0)  16.8 us
    all_gather x1, blocking collectives, on_device(): lax.all_gather(block, 'col', axis=0, tiled=True)  16.3 us
  transfers between devices with their start and end apart: 4, of which 1 were waited for; matrix products, arithmetic and copies ran while one was open for 17% of the time, Pallas kernels for 0%

profile of v1, /device:TPU:0, one launch (start us, length us, event | category | flops | bytes accessed | tf_op | source)
XLA Modules:
  0.0 325.5 jit_solution(1854546519629442459)
XLA Ops:
  8.0 16.3 %all-gather.4 = f32[8,576,16]{1,2,0:T(8,128)S(1)} all-gather(f32[1,576,16]{1,2,0:T(8,128)} %bitcast.97), channel_id=1, replica_groups=mesh['row'=4,'col'=8] {'col'}, dimensions={0}, use_global_device_ids=true | all-gather | bytes 331776 | tf_op jit(solution)/shard_map/all_gather | solution.py:20
  24.6 40.0 %fusion.44 = f32[4,576,16]{1,2,0:T(8,128)} fusion(f32[4,576,4608]{2,1,0:T(8,128)} %param.6, f32[4608,16,1]{0,1,2:T(8,128)S(1)} %reshape.48), kind=kOutput, calls=%fused_computation.77 | convolution fusion | flops 2038431744 | bytes 42909696 | tf_op jit(solution)/shard_map/aig,gk->aik/dot_general | solution.py:32
  64.9 8.8 %all-gather.5 = f32[4,576,16]{1,2,0:T(8,128)S(1)} all-gather(f32[1,576,16]{1,2,0:T(8,128)S(1)} %dynamic-slice_bitcast_fusion.2), channel_id=1, replica_groups=mesh['row'=4,'col'=8] {'row'}, dimensions={0}, use_global_device_ids=true | all-gather | bytes 184320 | tf_op jit(solution)/shard_map/all_gather | solution.py:29
  73.6 24.6 %convolution_bitcast_fusion.3 = f32[4608,16]{0,1:T(8,128)} fusion(f32[4,576,16]{1,2,0:T(8,128)S(1)} %all-gather.5, f32[4,576,4608]{2,1,0:T(8,128)} %param.6), kind=kOutput, calls=%fused_computation.9 | convolution fusion | flops 2038431744 | bytes 42909696 | tf_op jit(solution)/shard_map/aig,aik->gk/dot_general | solution.py:37
  99.9 27.3 %all-reduce = f32[4608]{0:T(1024)S(1)} all-reduce(f32[4608]{0:T(1024)S(1)} %dynamic-update-slice.2), channel_id=1, replica_groups=mesh['row'=4,'col'=8] {'col'}, use_global_device_ids=true, to_apply=%add | all-reduce | flops 4608 | bytes 36864
  127.2 0.9 copy.18
  128.2 24.6 %all-gather = f32[1,4608,16]{2,0,1:T(1,128)S(1)} all-gather(f32[1,576,16]{2,0,1:T(1,128)S(1)} %copy.18), channel_id=2, replica_groups=mesh['row'=4,'col'=8] {'col'}, dimensions={1}, use_global_device_ids=true | all-gather | bytes 331776 | tf_op jit(solution)/shard_map/all_gather | solution.py:39
  152.7 2.2 copy.19
  154.9 1.0 fusion.19
  156.0 0.9 fusion.5
  156.9 8.5 %all-gather.1 = f32[192,48]{1,0:T(8,128)S(1)} all-gather(f32[48,48]{1,0:T(8,128)S(1)} %fusion.5), channel_id=3, replica_groups=mesh['row'=4,'col'=8] {'row'}, dimensions={0}, use_global_device_ids=true | all-gather | bytes 46080 | tf_op jit(solution)/shard_map/all_gather | solution.py:12
  165.4 0.7 slice_bitcast_fusion.1
  166.7 1.5 cholesky.44
  168.2 0.6 compare_reduce_fusion.1
  168.9 0.6 fusion.37
  169.5 1.2 custom-call.6
  171.8 39.3 %convolution_bitcast_fusion.4 = f32[4,576,16]{1,2,0:T(8,128)} fusion(f32[4,576,4608]{2,1,0:T(8,128)} %param.6, f32[16,4608]{1,0:T(8,128)S(1)} %fusion.23), kind=kOutput, calls=%fused_computation.10 | convolution fusion | flops 2038431744 | bytes 42909696 | tf_op jit(solution)/shard_map/aig,gk->aik/dot_general | solution.py:32
  211.2 8.0 %all-gather.6 = f32[4,576,16]{1,2,0:T(8,128)S(1)} all-gather(f32[1,576,16]{1,2,0:T(8,128)S(1)} %dynamic-slice_bitcast_fusion.1), channel_id=1, replica_groups=mesh['row'=4,'col'=8] {'row'}, dimensions={0}, use_global_device_ids=true | all-gather | bytes 184320 | tf_op jit(solution)/shard_map/all_gather | solution.py:29
  219.3 24.6 %convolution_bitcast_fusion.2 = f32[4608,16]{0,1:T(8,128)} fusion(f32[4,576,16]{1,2,0:T(8,128)S(1)} %all-gather.6, f32[4,576,4608]{2,1,0:T(8,128)} %param.6), kind=kOutput, calls=%fused_computation.8 | convolution fusion | flops 2038431744 | bytes 42909696 | tf_op jit(solution)/shard_map/aig,aik->gk/dot_general | solution.py:37
  243.9 0.9 copy.23
  244.8 28.0 %all-gather.2 = f32[1,4608,16]{2,0,1:T(1,128)S(1)} all-gather(f32[1,576,16]{2,0,1:T(1,128)S(1)} %copy.23), channel_id=4, replica_groups=mesh['row'=4,'col'=8] {'col'}, dimensions={1}, use_global_device_ids=true | all-gather | bytes 331776 | tf_op jit(solution)/shard_map/all_gather | solution.py:39
  272.8 2.2 copy.24
  275.0 24.6 %all-reduce.8.cloned.1.call-done = f32[4608,16]{0,1:T(8,128)} async-done(((f32[4608,16]{0,1:T(8,128)}), f32[4608,16]{0,1:T(8,128)}) %all-reduce.8.cloned.1.call-update) | async-done | bytes 294928 | tf_op jit(solution)/shard_map/psum | solution.py:38
  299.6 1.1 fusion.17
  300.6 0.8 fusion.10
  301.5 8.3 %all-gather.3 = f32[192,48]{1,0:T(8,128)S(1)} all-gather(f32[48,48]{1,0:T(8,128)S(1)} %fusion.10), channel_id=5, replica_groups=mesh['row'=4,'col'=8] {'row'}, dimensions={0}, use_global_device_ids=true | all-gather | bytes 46080 | tf_op jit(solution)/shard_map/all_gather | solution.py:12
  311.1 1.5 cholesky.55
  312.6 0.6 compare_reduce_fusion
  313.2 0.6 fusion.36
  313.9 1.2 custom-call.7
  316.1 0.7 dynamic-slice_bitcast_fusion
  316.8 1.3 pad_maximum_fusion
  (52 shorter events, 5.6 us)
Async XLA Ops:
  8.0 119.2 %reduce-scatter.7.cloned.1.call-start = ((), (), s32[]{:S(2)}) async-start(), calls=%async_computation.4 | async-start | bytes 204800
  24.5 73.8 %copy-start.2 = (u32[32]{0:T(128)S(1)}, u32[32]{0:T(128)}, u32[]{:S(2)}) copy-start(u32[32]{0:T(128)} %constant.51) | copy-start | bytes 388
  24.5 75.1 %copy-start.1 = (f32[576]{0:T(1024)S(1)}, f32[576]{0:T(1024)}, u32[]{:S(2)}) copy-start(f32[576]{0:T(1024)} %param.7) | copy-start | bytes 6916
  64.6 90.3 %all-reduce.6.cloned.1.call-start = ((), (), s32[]{:S(2)}) async-start(), calls=%async_computation.2 | async-start | bytes 589824 | tf_op jit(solution)/shard_map/psum | solution.py:38
  98.3 145.6 %reduce-scatter.9.cloned.1.call-start = ((), (), s32[]{:S(2)}) async-start(), calls=%async_computation.5 | async-start | bytes 204800
  127.2 116.6 %copy-start = (f32[4608]{0:T(1024)}, f32[4608]{0:T(1024)S(1)}, u32[]{:S(2)}) copy-start(f32[4608]{0:T(1024)S(1)} %all-reduce) | copy-start | bytes 55300
  211.2 88.4 %all-reduce.8.cloned.1.call-start = ((), (), s32[]{:S(2)}) async-start(), calls=%async_computation.3 | async-start | bytes 589824 | tf_op jit(solution)/shard_map/psum | solution.py:38
Sparse Core Ops, SparseCore 0:
  64.7 25.2 reduce-scatter.6
  211.3 24.4 reduce-scatter.8
Sparse Core Ops, SparseCore 1:
  98.3 55.3 all-reduce.5
  244.0 55.6 all-reduce.7
